TPU v7x, 32 devices: a whole 2x2x4 slice. The times are simulated.
32 devices in a mesh: facet: 4 (over y, x), band: 4 (over z), sub: 2 (over core).
Axes of the slice: x: 2, y: 2, z: 4, core: 2. Of those that a mesh axis runs over, the one named last changes fastest.
Arguments:
- facets: bfloat16 [8192, 2048], P(('facet', 'band')), may hold values from -6 to 6
- window: float32 [2048], replicated, may hold values from 0.5 to 1.5
- facet_offsets: int32 [4, 2], replicated, may hold values from 0 to 49151
- row_offsets: int32 [8], replicated, may hold values from 0 to 49151
- column_offset: int32 [1], replicated, may hold values from 0 to 49151
- kernel: bfloat16 [256, 256], replicated, may hold values from -0.375 to 0.375
- tile_counts: int32 [8, 16, 16], replicated, may hold values from 0 to 32
Outputs:
- residual: bfloat16 [8192, 2048], P(('facet', 'band'))
All inputs are finite; a program needn't handle non-finite values.
Results may differ from a plain program's by a relative error of at most 0.013.
Values may be sent and summed in bfloat16 or wider, within the bound.
A program may use at most 64 MiB of HBM per device.

v0:
```python
import math
import jax
import jax.numpy as jnp
from jax import lax
from jax.sharding import PartitionSpec as P

IMAGE = 49152


def modular_product(first, second):
    upper_bits = first // 256
    lower_bits = first % 256
    reduced = upper_bits * second % IMAGE
    reduced = reduced * 256 % IMAGE
    return (reduced + lower_bits * second) % IMAGE


def phase_table(frequency, position):
    reduced = modular_product(frequency % IMAGE, position % IMAGE)
    angle = reduced.astype(jnp.float32) * (2.0 * math.pi / IMAGE)
    return (jnp.cos(angle), jnp.sin(angle))


def product(left, right):
    return jnp.dot(left, right, preferred_element_type=jnp.float32)


def body(facets, window, facet_offsets, row_offsets, column_offset, kernel, tile_counts):
    facet_count = lax.axis_size("facet")
    band_count = lax.axis_size("band")
    sub_count = lax.axis_size("sub")
    facet_at = lax.axis_index("facet")
    band_at = lax.axis_index("band")
    sub_at = lax.axis_index("sub")
    band_rows = facets.shape[0]
    width = facets.shape[1]
    contrib = kernel.shape[0]
    sub_rows = contrib // band_count
    stacked = band_count * contrib
    a_scale = 1.0 / math.sqrt(width * facet_count)
    b_scale = 1.0 / math.sqrt(width)
    back_scale = 1.0 / math.sqrt(band_count * sub_count * contrib)
    out_scale = 1.0 / math.sqrt(contrib)
    offset = lax.dynamic_slice_in_dim(facet_offsets, facet_at, 1, 0)[0]
    cells = jnp.arange(width, dtype=jnp.int32)
    frequencies = jnp.arange(contrib, dtype=jnp.int32)
    cosine, sine = phase_table(column_offset[0] + frequencies[:, None], offset[1] + cells[None, :])
    col_real = (cosine * window[None, :] * b_scale).astype(jnp.bfloat16)
    col_imag = (-sine * window[None, :] * b_scale).astype(jnp.bfloat16)
    t_real = jnp.einsum("xy,ky->xk", facets, col_real, preferred_element_type=jnp.float32).astype(
        jnp.bfloat16
    )
    t_imag = jnp.einsum("xy,ky->xk", facets, col_imag, preferred_element_type=jnp.float32).astype(
        jnp.bfloat16
    )
    starts = lax.dynamic_slice_in_dim(row_offsets, sub_at * band_count, band_count, 0)
    row_freqs = (starts[:, None] + frequencies[None, :]).reshape(stacked)
    positions = offset[0] + band_at * band_rows + jnp.arange(band_rows, dtype=jnp.int32)
    row_cos, row_sin = phase_table(row_freqs[:, None], positions[None, :])
    a_real = (row_cos * a_scale).astype(jnp.bfloat16)
    a_imag = (-row_sin * a_scale).astype(jnp.bfloat16)
    part_real = product(a_real, t_real) - product(a_imag, t_imag)
    part_imag = product(a_real, t_imag) + product(a_imag, t_real)
    terms = jnp.stack([part_real, part_imag]).reshape(2, band_count, band_count, sub_rows, contrib)
    blocks = lax.psum_scatter(
        terms.astype(jnp.bfloat16), "band", scatter_dimension=2, tiled=True
    ).astype(jnp.float32)
    blocks = lax.psum(blocks, "facet")
    grid_part = blocks.reshape(2, band_count, sub_rows, contrib).astype(jnp.bfloat16)
    tiles = tile_counts.shape[1]
    tile_side = contrib // tiles
    counts = lax.dynamic_slice_in_dim(tile_counts, sub_at * band_count, band_count, 0).astype(
        jnp.float32
    )
    ratio = counts / (counts + 4.0)
    weights = jnp.broadcast_to(
        ratio[:, :, None, :, None], (band_count, tiles, tile_side, tiles, tile_side)
    )
    weights = weights.reshape(band_count, contrib, contrib)
    y_cols = jnp.einsum(
        "ij,cgrj->cgir", kernel, grid_part, preferred_element_type=jnp.float32
    ).astype(jnp.bfloat16)
    y_cols = lax.all_to_all(y_cols, "band", split_axis=2, concat_axis=3, tiled=True)
    z_cols = jnp.einsum("cgqi,ji->cgqj", y_cols, kernel, preferred_element_type=jnp.float32)
    weight_cols = jnp.swapaxes(
        lax.dynamic_slice_in_dim(weights, band_at * sub_rows, sub_rows, 2), 1, 2
    )
    w_cols = (weight_cols[None] * z_cols).astype(jnp.bfloat16)
    u_cols = jnp.einsum("cgqj,jl->cgql", w_cols, kernel, preferred_element_type=jnp.float32).astype(
        jnp.bfloat16
    )
    u_back = lax.all_to_all(u_cols, "band", split_axis=3, concat_axis=2, tiled=True)
    residual_grid = jnp.einsum(
        "cgqr,qm->cgrm", u_back, kernel, preferred_element_type=jnp.float32
    ).astype(jnp.bfloat16)
    back_real = (row_cos * back_scale).astype(jnp.bfloat16).reshape(band_count, contrib, band_rows)
    back_imag = (row_sin * back_scale).astype(jnp.bfloat16).reshape(band_count, contrib, band_rows)
    piece = lax.all_gather(residual_grid, "band", axis=2, tiled=True)
    e_real = jnp.einsum("gkx,gkl->xl", back_real, piece[0], preferred_element_type=jnp.float32)
    e_real = e_real - jnp.einsum(
        "gkx,gkl->xl", back_imag, piece[1], preferred_element_type=jnp.float32
    )
    e_imag = jnp.einsum("gkx,gkl->xl", back_real, piece[1], preferred_element_type=jnp.float32)
    e_imag = e_imag + jnp.einsum(
        "gkx,gkl->xl", back_imag, piece[0], preferred_element_type=jnp.float32
    )
    e_real, e_imag = (e_real, e_imag)
    e_real, e_imag = (
        lax.psum(e_real.astype(jnp.bfloat16), "sub").astype(jnp.float32),
        lax.psum(e_imag.astype(jnp.bfloat16), "sub").astype(jnp.float32),
    )
    out_cos = (cosine * out_scale).astype(jnp.bfloat16)
    out_sin = (sine * out_scale).astype(jnp.bfloat16)
    image = product(e_real.astype(jnp.bfloat16), out_cos) - product(
        e_imag.astype(jnp.bfloat16), out_sin
    )
    return (window[None, :] * image).astype(jnp.bfloat16)


def solution(mesh):
    in_specs = (P(("facet", "band"), None), P(), P(), P(), P(), P(), P())
    out_specs = P(("facet", "band"), None)
    return jax.shard_map(body, mesh=mesh, in_specs=in_specs, out_specs=out_specs, check_vma=False)
```

profile of v0, /device:TPU:0, one launch (start us, length us, event | category | flops | bytes accessed | tf_op | source)
XLA Modules:
  0.0 311.3 jit_solution(18280598410825204298)
XLA Ops:
  7.3 0.8 constant_dynamic-slice_fusion
  8.1 0.5 fusion.138
  8.7 0.7 add_select_fusion.9
  9.3 12.9 %convolution_convert_fusion.3 = bf16[256,512]{1,0:T(8,128)(2,1)} fusion(bf16[512,2048]{1,0:T(8,128)(2,1)S(1)} %copy-done, f32[2048]{0:T(1024)} %param.8, s32[256]{0:T(256)S(1)} %get-tuple-element.14, s32[2048]{0:T(1024)S(1)} %add_select_fusion.9, s32[256]{0:T(256)S(1)} %get-tuple-element.15), kind=kOutput, calls=%fused_computation.73 | convolution fusion | flops 551682048 | bytes 2377728 | tf_op jit(solution)/shard_map/xy,ky->xk/dot_general | solution.py:53
  22.3 10.5 %convolution_convert_fusion.4 = bf16[256,512]{1,0:T(8,128)(2,1)S(1)} fusion(bf16[512,2048]{1,0:T(8,128)(2,1)S(1)} %copy-done, f32[2048]{0:T(1024)S(1)} %copy-done.11, s32[256]{0:T(256)S(1)} %get-tuple-element.14, s32[2048]{0:T(1024)S(1)} %add_select_fusion.9, s32[256]{0:T(256)S(1)} %get-tuple-element.15), kind=kOutput, calls=%fused_computation.74 | convolution fusion | flops 551157760 | bytes 2377728 | tf_op jit(solution)/shard_map/xy,ky->xk/dot_general | solution.py:50
  33.6 10.6 %fusion.58 = f32[1024,256]{1,0:T(8,128)S(1)} fusion(bf16[256,512]{1,0:T(8,128)(2,1)S(1)} %convolution_convert_fusion.4, s32[1024]{0:T(1024)S(1)} %get-tuple-element.8, s32[512]{0:T(512)S(1)} %add_select_fusion.16, s32[1024]{0:T(1024)S(1)} %get-tuple-element.7), kind=kOutput, calls=%fused_computation.88 | convolution fusion | flops 282066944 | bytes 1320960 | tf_op jit(solution)/shard_map/dot_general | solution.py:25
  44.2 10.7 %fusion.57 = f32[1024,256]{1,0:T(8,128)S(1)} fusion(bf16[256,512]{1,0:T(8,128)(2,1)S(1)} %copy-done.14, s32[1024]{0:T(1024)S(1)} %get-tuple-element.8, s32[512]{0:T(512)S(1)} %add_select_fusion.16, s32[1024]{0:T(1024)S(1)} %get-tuple-element.7), kind=kOutput, calls=%fused_computation.87 | convolution fusion | flops 282066944 | bytes 1320960 | tf_op jit(solution)/shard_map/dot_general | solution.py:25
  54.9 11.6 %fusion.36 = bf16[1024,256]{1,0:T(8,128)(2,1)S(1)} fusion(f32[1024,256]{1,0:T(8,128)S(1)} %fusion.58, bf16[256,512]{1,0:T(8,128)(2,1)S(1)} %copy-done.14, s32[1024]{0:T(1024)S(1)} %get-tuple-element.8, s32[512]{0:T(512)S(1)} %add_select_fusion.16, s32[1024]{0:T(1024)S(1)} %get-tuple-element.7), kind=kOutput, calls=%fused_computation.59 | convolution fusion | flops 283115520 | bytes 1845248 | tf_op jit(solution)/shard_map/dot_general | solution.py:25
  66.5 12.0 %fusion.37 = bf16[1024,256]{1,0:T(8,128)(2,1)S(1)} fusion(f32[1024,256]{1,0:T(8,128)S(1)} %fusion.57, bf16[256,512]{1,0:T(8,128)(2,1)S(1)} %convolution_convert_fusion.4, s32[1024]{0:T(1024)S(1)} %get-tuple-element.8, s32[512]{0:T(512)S(1)} %add_select_fusion.16, s32[1024]{0:T(1024)S(1)} %get-tuple-element.7), kind=kOutput, calls=%fused_computation.60 | convolution fusion | flops 283115520 | bytes 1845248 | tf_op jit(solution)/shard_map/dot_general | solution.py:25
  78.6 1.0 copy.25
  79.8 30.1 %reduce-scatter.2.cloned.1.call-done = bf16[2,4,1,64,256]{4,3,1,0,2:T(8,128)(2,1)} async-done(((bf16[2,4,4,64,256]{4,3,1,0,2:T(8,128)(2,1)}), bf16[2,4,1,64,256]{4,3,1,0,2:T(8,128)(2,1)}) %reduce-scatter.2.cloned.1.call-update) | async-done | bytes 262160 | tf_op jit(solution)/shard_map/reduce_scatter | solution.py:65
  109.9 44.5 %all-reduce.4.cloned.1.call-done = bf16[2,4,1,64,256]{4,3,1,0,2:T(8,128)(2,1)} async-done(((bf16[2,4,1,64,256]{4,3,1,0,2:T(8,128)(2,1)}), bf16[2,4,1,64,256]{4,3,1,0,2:T(8,128)(2,1)}) %all-reduce.4.cloned.1.call-update) | async-done | bytes 262160 | tf_op jit(solution)/shard_map/psum | solution.py:68
  154.4 1.2 fusion.43
  155.9 1.1 reshape.290
  157.0 4.6 %all-to-all-start = ((bf16[4,2,16384]{2,1,0:T(2,128)(2,1)}), bf16[4,2,16384]{2,1,0:T(2,128)(2,1)S(1)}, u32[]{:S(2)}, u32[]{:S(2)}) async-start(bf16[4,2,16384]{2,1,0:T(2,128)(2,1)} %reshape.290), calls=%async_computation.1 | async-start | bytes 524288 | tf_op jit(solution)/shard_map/all_to_all | solution.py:83
  161.7 3.9 %broadcast_in_dim.2 = f32[4,16,16,16,16]{2,1,4,3,0:T(8,128)} broadcast(f32[4,16,16]{1,2,0:T(8,128)S(1)} %copy.17), dimensions={0,1,3} | broadcast | bytes 1052672 | tf_op jit(solution)/shard_map/broadcast_in_dim | solution.py:76
  165.6 6.1 %reshape.284 = f32[4,256,256]{1,2,0:T(8,128)S(1)} reshape(f32[4,16,16,16,16]{2,1,4,3,0:T(8,128)} %broadcast_in_dim.2) | data formatting | bytes 2097152 | tf_op jit(solution)/shard_map/reshape | solution.py:79
  171.7 0.7 dynamic-slice_bitcast_fusion
  172.8 0.4 copy.30
  173.6 1.4 convolution_convert_fusion.1
  175.3 0.4 reshape.292
  175.7 12.7 %all_to_all.36 = bf16[4,2,16384]{2,1,0:T(2,128)(2,1)S(1)} all-to-all(bf16[4,2,16384]{2,1,0:T(2,128)(2,1)S(1)} %reshape.292), channel_id=1, replica_groups=mesh['facet'=4,'band'=4,'sub'=2] {'band'}, dimensions={0} | all-to-all | bytes 524288 | tf_op jit(solution)/shard_map/all_to_all | solution.py:92
  188.8 0.4 copy.29
  189.5 0.9 convolution_convert_fusion
  190.7 26.0 %all-gather.2.cloned.1.call-done = bf16[2,4,256,256]{3,2,1,0:T(8,128)(2,1)} async-done(((bf16[2,4,64,256]{3,2,1,0:T(8,128)(2,1)}), bf16[2,4,256,256]{3,2,1,0:T(8,128)(2,1)}) %all-gather.2.cloned.1.call-update) | async-done | bytes 1048592 | tf_op jit(solution)/shard_map/all_gather | solution.py:98
  216.7 11.7 %convolution_bitcast_fusion = f32[512,256]{1,0:T(8,128)S(1)} fusion(s32[4,256]{1,0:T(4,128)S(1)} %get-tuple-element.12, s32[512]{0:T(512)S(1)} %copy-done.4, s32[4,256]{1,0:T(4,128)S(1)} %get-tuple-element.13, bf16[2,4,256,256]{3,2,1,0:T(8,128)(2,1)} %all-gather.2.cloned.1.call-done), kind=kOutput, calls=%fused_computation.61 | convolution fusion | flops 282066944 | bytes 1058816 | tf_op jit(solution)/shard_map/gkx,gkl->xl/dot_general | solution.py:104
  228.4 10.8 %convolution_bitcast_fusion.2 = f32[512,256]{1,0:T(8,128)S(1)} fusion(s32[4,256]{1,0:T(4,128)S(1)} %get-tuple-element.12, s32[512]{0:T(512)S(1)} %copy-done.4, s32[4,256]{1,0:T(4,128)S(1)} %get-tuple-element.13, bf16[2,4,256,256]{3,2,1,0:T(8,128)(2,1)S(1)} %copy-done.9), kind=kOutput, calls=%fused_computation.63 | convolution fusion | flops 282066944 | bytes 1058816 | tf_op jit(solution)/shard_map/gkx,gkl->xl/dot_general | solution.py:100
  239.2 11.6 %fusion.40 = bf16[512,256]{1,0:T(8,128)(2,1)} fusion(f32[512,256]{1,0:T(8,128)S(1)} %convolution_bitcast_fusion, s32[4,256]{1,0:T(4,128)S(1)} %get-tuple-element.12, s32[512]{0:T(512)S(1)} %copy-done.4, s32[4,256]{1,0:T(4,128)S(1)} %get-tuple-element.13, bf16[2,4,256,256]{3,2,1,0:T(8,128)(2,1)S(1)} %copy-done.9), kind=kOutput, calls=%fused_computation.68 | convolution fusion | flops 282329088 | bytes 1320960 | tf_op jit(solution)/shard_map/gkx,gkl->xl/dot_general | solution.py:103
  250.7 11.4 %fusion.41 = bf16[512,256]{1,0:T(8,128)(2,1)} fusion(f32[512,256]{1,0:T(8,128)S(1)} %convolution_bitcast_fusion.2, s32[4,256]{1,0:T(4,128)S(1)} %get-tuple-element.12, s32[512]{0:T(512)S(1)} %copy-done.4, s32[4,256]{1,0:T(4,128)S(1)} %get-tuple-element.13, bf16[2,4,256,256]{3,2,1,0:T(8,128)(2,1)S(1)} %copy-done.9), kind=kOutput, calls=%fused_computation.69 | convolution fusion | flops 282329088 | bytes 1320960 | tf_op jit(solution)/shard_map/gkx,gkl->xl/dot_general | solution.py:99
  262.1 18.2 %all-reduce.6.cloned.1.call-done = (bf16[512,256]{1,0:T(8,128)(2,1)}, bf16[512,256]{1,0:T(8,128)(2,1)}) async-done(((bf16[512,256]{1,0:T(8,128)(2,1)}, bf16[512,256]{1,0:T(8,128)(2,1)}), (bf16[512,256]{1,0:T(8,128)(2,1)}, bf16[512,256]{1,0:T(8,128)(2,1)})) %all-reduce.6.cloned.1.call-update) | async-done | bytes 524304 | tf_op jit(solution)/shard_map/psum | solution.py:109
  280.4 11.8 %fusion.44 = f32[512,2048]{1,0:T(8,128)S(1)} fusion(bf16[512,256]{1,0:T(8,128)(2,1)} %get-tuple-element.5, s32[256]{0:T(256)S(1)} %copy-done.6, s32[2048]{0:T(1024)S(1)} %add_select_fusion.9, s32[256]{0:T(256)S(1)} %copy-done.8), kind=kOutput, calls=%fused_computation.77 | convolution fusion | flops 550502400 | bytes 4466688 | tf_op jit(solution)/shard_map/dot_general | solution.py:25
  292.1 12.3 %multiply_convert_fusion = bf16[512,2048]{1,0:T(8,128)(2,1)} fusion(f32[512,2048]{1,0:T(8,128)S(1)} %fusion.44, bf16[512,256]{1,0:T(8,128)(2,1)S(1)} %copy-done.10, f32[2048]{0:T(1024)S(1)} %copy-done.12, s32[256]{0:T(256)S(1)} %copy-done.6, s32[2048]{0:T(1024)S(1)} %add_select_fusion.9, s32[256]{0:T(256)S(1)} %copy-done.8), kind=kOutput, calls=%fused_computation | convolution fusion | flops 553648128 | bytes 6572032 | tf_op jit(solution)/shard_map/dot_general | solution.py:25
  (54 shorter events, 2.8 us)
Async XLA Ops:
  6.5 2.8 copy-start
  6.5 103.3 %reduce-scatter.2.cloned.1.call-start = ((), (), s32[]{:S(2)}) async-start(), calls=%async_computation.3 | async-start | bytes 1310720 | tf_op jit(solution)/shard_map/reduce_scatter | solution.py:65
  8.6 13.6 %copy-start.5 = (s32[256]{0:T(256)}, s32[256]{0:T(256)S(1)}, u32[]{:S(2)}) copy-start(s32[256]{0:T(256)S(1)} %get-tuple-element.14) | copy-start | bytes 3076
  8.6 13.6 %copy-start.7 = (s32[256]{0:T(256)}, s32[256]{0:T(256)S(1)}, u32[]{:S(2)}) copy-start(s32[256]{0:T(256)S(1)} %get-tuple-element.15) | copy-start | bytes 3076
  9.3 12.9 %copy-start.11 = (f32[2048]{0:T(1024)S(1)}, f32[2048]{0:T(1024)}, u32[]{:S(2)}) copy-start(f32[2048]{0:T(1024)} %param.8) | copy-start | bytes 24580
  22.3 11.1 %copy-start.13 = (s32[8]{0:T(128)S(1)}, s32[8]{0:T(128)}, u32[]{:S(2)}) copy-start(s32[8]{0:T(128)} %param.10) | copy-start | bytes 100
  33.4 33.1 %copy-start.3 = (s32[512]{0:T(512)}, s32[512]{0:T(512)S(1)}, u32[]{:S(2)}) copy-start(s32[512]{0:T(512)S(1)} %add_select_fusion.16) | copy-start | bytes 6148
  33.6 10.6 %copy-start.14 = (bf16[256,512]{1,0:T(8,128)(2,1)S(1)}, bf16[256,512]{1,0:T(8,128)(2,1)}, u32[]{:S(2)}) copy-start(bf16[256,512]{1,0:T(8,128)(2,1)} %convolution_convert_fusion.3) | copy-start | bytes 786436
  78.6 75.8 %copy-start.1 = (bf16[256,256]{1,0:T(8,128)(2,1)S(1)}, bf16[256,256]{1,0:T(8,128)(2,1)}, u32[]{:S(2)}) copy-start(bf16[256,256]{1,0:T(8,128)(2,1)} %param.12) | copy-start | bytes 393220
  79.7 82.0 %copy-start.2 = (s32[8,16,16]{2,1,0:T(8,128)S(1)}, s32[8,16,16]{2,1,0:T(8,128)}, u32[]{:S(2)}) copy-start(s32[8,16,16]{2,1,0:T(8,128)} %param.13) | copy-start | bytes 24580
  79.7 74.7 %all-reduce.4.cloned.1.call-start = ((), (), s32[]{:S(2)}) async-start(), calls=%async_computation.4 | async-start | bytes 524288 | tf_op jit(solution)/shard_map/psum | solution.py:68
  157.0 15.4 %all-to-all-start = ((bf16[4,2,16384]{2,1,0:T(2,128)(2,1)}), bf16[4,2,16384]{2,1,0:T(2,128)(2,1)S(1)}, u32[]{:S(2)}, u32[]{:S(2)}) async-start(bf16[4,2,16384]{2,1,0:T(2,128)(2,1)} %reshape.290), calls=%async_computation.1 | async-start | bytes 524288 | tf_op jit(solution)/shard_map/all_to_all | solution.py:83
  161.6 55.1 %all-gather.2.cloned.1.call-start = ((), (), s32[]{:S(2)}) async-start(), calls=%async_computation.5 | async-start | bytes 1310720 | tf_op jit(solution)/shard_map/all_gather | solution.py:98
  175.7 41.1 %copy-start.4 = (s32[512]{0:T(512)S(1)}, s32[512]{0:T(512)}, u32[]{:S(2)}) copy-start(s32[512]{0:T(512)} %copy-done.3) | copy-start | bytes 6148
  190.5 89.9 %all-reduce.6.cloned.1.call-start = ((), (), s32[]{:S(2)}) async-start(), calls=%async_computation.6 | async-start | bytes 1048576 | tf_op jit(solution)/shard_map/psum | solution.py:109
  216.7 11.7 %copy-start.9 = (bf16[2,4,256,256]{3,2,1,0:T(8,128)(2,1)S(1)}, bf16[2,4,256,256]{3,2,1,0:T(8,128)(2,1)}, u32[]{:S(2)}) copy-start(bf16[2,4,256,256]{3,2,1,0:T(8,128)(2,1)} %all-gather.2.cloned.1.call-done) | copy-start | bytes 3145732
  250.7 29.6 %copy-start.6 = (s32[256]{0:T(256)S(1)}, s32[256]{0:T(256)}, u32[]{:S(2)}) copy-start(s32[256]{0:T(256)} %copy-done.5) | copy-start | bytes 3076
  250.7 29.6 %copy-start.8 = (s32[256]{0:T(256)S(1)}, s32[256]{0:T(256)}, u32[]{:S(2)}) copy-start(s32[256]{0:T(256)} %copy-done.7) | copy-start | bytes 3076
  280.3 11.8 %copy-start.10 = (bf16[512,256]{1,0:T(8,128)(2,1)S(1)}, bf16[512,256]{1,0:T(8,128)(2,1)}, u32[]{:S(2)}) copy-start(bf16[512,256]{1,0:T(8,128)(2,1)} %get-tuple-element.6) | copy-start | bytes 786436
  280.3 11.8 %copy-start.12 = (f32[2048]{0:T(1024)S(1)}, f32[2048]{0:T(1024)}, u32[]{:S(2)}) copy-start(f32[2048]{0:T(1024)} %param.8) | copy-start | bytes 24580
Sparse Core Ops, SparseCore 0:
  79.8 29.9 reduce-scatter.1
  112.8 41.5 all-reduce.3
  190.6 26.0 all-gather.1
  262.3 18.0 all-reduce.5
where the time goes:
time: 316 us; the launch traced here: 311 us
  matrix products  141 us (45%)
  waiting for transfers between devices  119 us (38%)
  local copies, waits for them, and re-layouts  17.5 us (6%)
  between operations  15.1 us (5%)
  blocking collectives  12.7 us (4%)
  starting transfers between devices  4.85 us (2%)
    dot_general x6, matrix products, product(): return jnp.dot(left, right, preferred_element_type=jnp.float32)  69 us
    psum x1, waiting for transfers between devices, body(): blocks = lax.psum(blocks, 'facet')  44.5 us
    reduce_scatter x1, waiting for transfers between devices, body(): lax.psum_scatter(terms.astype(jnp.bfloat16), 'band', scatter_dimension=2,...  30.1 us
    all_gather x1, waiting for transfers between devices, body(): piece = lax.all_gather(residual_grid, 'band', axis=2, tiled=True)  26 us
    psum x1, waiting for transfers between devices, body(): lax.psum(e_real.astype(jnp.bfloat16), 'sub').astype(jnp.float32)  18.2 us
    dot_general x1, matrix products, body(): jnp.einsum('xy,ky->xk', facets, col_imag, preferred_element_type=jnp.floa...  12.9 us
    all_to_all x1, blocking collectives, body(): lax.all_to_all(u_cols, 'band', split_axis=3, concat_axis=2, tiled=True)  12.7 us
    dot_general x1, matrix products, body(): jnp.einsum('gkx,gkl->xl', back_imag, piece[0], preferred_element_type=jnp...  11.7 us
  transfers between devices with their start and end apart: 5, of which 4 were waited for; matrix products, arithmetic and copies ran while one was open for 3% of the time, Pallas kernels for 0%

commit v1 on v0

--- a/solution.py
+++ b/solution.py
@@ -65,7 +65,12 @@
     blocks = lax.psum_scatter(
         terms.astype(jnp.bfloat16), "band", scatter_dimension=2, tiled=True
     ).astype(jnp.float32)
-    blocks = lax.psum(blocks, "facet")
+
+    def ends_set(axis_key, mine):
+        left_arr = lax.all_gather(mine, axis_key)
+        return jnp.sum(left_arr, axis=0)
+
+    blocks = ends_set("facet", blocks)
     grid_part = blocks.reshape(2, band_count, sub_rows, contrib).astype(jnp.bfloat16)
     tiles = tile_counts.shape[1]
     tile_side = contrib // tiles

time: 316 us -> 335 us (1.060)
  waiting for transfers between devices: 119 us -> 133 us
  other arithmetic: 0.95 us -> 6.15 us
    unnamed x4 -> x5, waiting for transfers between devices: 0.07 us -> 54.1 us
    psum x1 -> x0, waiting for transfers between devices: 44.5 us -> none  [body(): blocks = lax.psum(blocks, 'facet')]
    all_gather x0 -> x1, waiting for transfers between devices: none -> 34.6 us  [ends_set(): left_arr = lax.all_gather(mine, axis_key)]
    reduce_scatter x1 -> x0, waiting for transfers between devices: 30.1 us -> none  [body(): lax.psum_scatter(terms.astype(jnp.bfloat16), 'band', scatter_dimension=2,...]
where the time goes in v1:
time: 335 us; the launch traced here: 330 us
  matrix products  140 us (42%)
  waiting for transfers between devices  133 us (40%)
  local copies, waits for them, and re-layouts  17.2 us (5%)
  between operations  15.2 us (5%)
  blocking collectives  13 us (4%)
  other arithmetic  6.15 us (2%)
  starting transfers between devices  4.87 us (1%)
    dot_general x6, matrix products, product(): return jnp.dot(left, right, preferred_element_type=jnp.float32)  69 us
    unnamed x5, waiting for transfers between devices  54.1 us
    all_gather x1, waiting for transfers between devices, ends_set(): left_arr = lax.all_gather(mine, axis_key)  34.6 us
    all_gather x1, waiting for transfers between devices, body(): piece = lax.all_gather(residual_grid, 'band', axis=2, tiled=True)  26 us
    psum x1, waiting for transfers between devices, body(): lax.psum(e_real.astype(jnp.bfloat16), 'sub').astype(jnp.float32)  18.2 us
    all_to_all x1, blocking collectives, body(): lax.all_to_all(u_cols, 'band', split_axis=3, concat_axis=2, tiled=True)  13 us
    dot_general x1, matrix products, body(): jnp.einsum('xy,ky->xk', facets, col_imag, preferred_element_type=jnp.floa...  12.9 us
    dot_general x1, matrix products, body(): jnp.einsum('gkx,gkl->xl', back_imag, piece[0], preferred_element_type=jnp...  11.7 us
  transfers between devices with their start and end apart: 5, of which 4 were waited for; matrix products, arithmetic and copies ran while one was open for 3% of the time, Pallas kernels for 0%

profile of v1, /device:TPU:0, one launch (start us, length us, event | category | flops | bytes accessed | tf_op | source)
XLA Modules:
  0.0 329.7 jit_solution(7013215361662832762)
XLA Ops:
  7.3 0.8 constant_dynamic-slice_fusion
  8.1 0.6 fusion.137
  8.7 0.7 add_select_fusion.9
  9.4 12.9 %convolution_convert_fusion.3 = bf16[256,512]{1,0:T(8,128)(2,1)} fusion(bf16[512,2048]{1,0:T(8,128)(2,1)S(1)} %copy-done, f32[2048]{0:T(1024)} %param.8, s32[256]{0:T(256)S(1)} %get-tuple-element.14, s32[2048]{0:T(1024)S(1)} %add_select_fusion.9, s32[256]{0:T(256)S(1)} %get-tuple-element.15), kind=kOutput, calls=%fused_computation.73 | convolution fusion | flops 551682048 | bytes 2377728 | tf_op jit(solution)/shard_map/xy,ky->xk/dot_general | solution.py:53
  22.3 10.5 %convolution_convert_fusion.4 = bf16[256,512]{1,0:T(8,128)(2,1)S(1)} fusion(bf16[512,2048]{1,0:T(8,128)(2,1)S(1)} %copy-done, f32[2048]{0:T(1024)S(1)} %copy-done.11, s32[256]{0:T(256)S(1)} %get-tuple-element.14, s32[2048]{0:T(1024)S(1)} %add_select_fusion.9, s32[256]{0:T(256)S(1)} %get-tuple-element.15), kind=kOutput, calls=%fused_computation.74 | convolution fusion | flops 551157760 | bytes 2377728 | tf_op jit(solution)/shard_map/xy,ky->xk/dot_general | solution.py:50
  33.8 10.6 %fusion.58 = f32[1024,256]{1,0:T(8,128)S(1)} fusion(bf16[256,512]{1,0:T(8,128)(2,1)S(1)} %convolution_convert_fusion.4, s32[1024]{0:T(1024)S(1)} %get-tuple-element.8, s32[512]{0:T(512)S(1)} %add_select_fusion.16, s32[1024]{0:T(1024)S(1)} %get-tuple-element.7), kind=kOutput, calls=%fused_computation.88 | convolution fusion | flops 282066944 | bytes 1320960 | tf_op jit(solution)/shard_map/dot_general | solution.py:25
  44.4 10.7 %fusion.57 = f32[1024,256]{1,0:T(8,128)S(1)} fusion(bf16[256,512]{1,0:T(8,128)(2,1)S(1)} %copy-done.15, s32[1024]{0:T(1024)S(1)} %get-tuple-element.8, s32[512]{0:T(512)S(1)} %add_select_fusion.16, s32[1024]{0:T(1024)S(1)} %get-tuple-element.7), kind=kOutput, calls=%fused_computation.87 | convolution fusion | flops 282066944 | bytes 1320960 | tf_op jit(solution)/shard_map/dot_general | solution.py:25
  55.1 11.6 %fusion.36 = bf16[1024,256]{1,0:T(8,128)(2,1)S(1)} fusion(f32[1024,256]{1,0:T(8,128)S(1)} %fusion.58, bf16[256,512]{1,0:T(8,128)(2,1)S(1)} %copy-done.15, s32[1024]{0:T(1024)S(1)} %get-tuple-element.8, s32[512]{0:T(512)S(1)} %add_select_fusion.16, s32[1024]{0:T(1024)S(1)} %get-tuple-element.7), kind=kOutput, calls=%fused_computation.59 | convolution fusion | flops 283115520 | bytes 1845248 | tf_op jit(solution)/shard_map/dot_general | solution.py:25
  66.7 12.0 %fusion.37 = bf16[1024,256]{1,0:T(8,128)(2,1)S(1)} fusion(f32[1024,256]{1,0:T(8,128)S(1)} %fusion.57, bf16[256,512]{1,0:T(8,128)(2,1)S(1)} %convolution_convert_fusion.4, s32[1024]{0:T(1024)S(1)} %get-tuple-element.8, s32[512]{0:T(512)S(1)} %add_select_fusion.16, s32[1024]{0:T(1024)S(1)} %get-tuple-element.7), kind=kOutput, calls=%fused_computation.60 | convolution fusion | flops 283115520 | bytes 1845248 | tf_op jit(solution)/shard_map/dot_general | solution.py:25
  78.7 1.1 pad_maximum_fusion
  79.8 0.6 dynamic-slice
  80.5 54.1 %all-reduce.5.cloned.1.call-done = bf16[2,4,4,64,256]{4,3,2,1,0:T(8,128)(2,1)} async-done(((bf16[2,4,4,64,256]{4,3,2,1,0:T(8,128)(2,1)}), bf16[2,4,4,64,256]{4,3,2,1,0:T(8,128)(2,1)}) %all-reduce.5.cloned.1.call-update) | async-done | bytes 1048592
  134.6 2.4 dynamic-slice_convert_fusion
  137.0 34.6 %all-gather.6.cloned.1.call-done = f32[8,4,1,64,256]{4,3,2,1,0:T(8,128)} async-done(((f32[2,4,1,64,256]{4,3,2,1,0:T(8,128)}), f32[8,4,1,64,256]{4,3,2,1,0:T(8,128)}) %all-gather.6.cloned.1.call-update) | async-done | bytes 2097168 | tf_op jit(solution)/shard_map/all_gather | solution.py:70
  171.6 1.8 reduce.1
  174.0 1.1 reshape.297
  175.1 4.6 %all-to-all-start = ((bf16[4,2,16384]{2,1,0:T(2,128)(2,1)}), bf16[4,2,16384]{2,1,0:T(2,128)(2,1)S(1)}, u32[]{:S(2)}, u32[]{:S(2)}) async-start(bf16[4,2,16384]{2,1,0:T(2,128)(2,1)} %reshape.297), calls=%async_computation | async-start | bytes 524288 | tf_op jit(solution)/shard_map/all_to_all | solution.py:88
  179.8 3.9 %broadcast_in_dim.2 = f32[4,16,16,16,16]{2,1,4,3,0:T(8,128)} broadcast(f32[4,16,16]{1,2,0:T(8,128)S(1)} %copy.13), dimensions={0,1,3} | broadcast | bytes 1052672 | tf_op jit(solution)/shard_map/broadcast_in_dim | solution.py:81
  183.7 6.1 %reshape.285 = f32[4,256,256]{1,2,0:T(8,128)S(1)} reshape(f32[4,16,16,16,16]{2,1,4,3,0:T(8,128)} %broadcast_in_dim.2) | data formatting | bytes 2097152 | tf_op jit(solution)/shard_map/reshape | solution.py:84
  189.8 0.7 dynamic-slice_bitcast_fusion
  190.9 0.4 copy.25
  191.6 1.4 convolution_convert_fusion.1
  193.8 13.0 %all_to_all.36 = bf16[4,2,16384]{2,1,0:T(2,128)(2,1)S(1)} all-to-all(bf16[4,2,16384]{2,1,0:T(2,128)(2,1)S(1)} %reshape.299), channel_id=1, replica_groups=mesh['facet'=4,'band'=4,'sub'=2] {'band'}, dimensions={0} | all-to-all | bytes 524288 | tf_op jit(solution)/shard_map/all_to_all | solution.py:97
  207.9 0.9 convolution_convert_fusion
  209.1 26.0 %all-gather.4.cloned.1.call-done = bf16[2,4,256,256]{3,2,1,0:T(8,128)(2,1)} async-done(((bf16[2,4,64,256]{3,2,1,0:T(8,128)(2,1)}), bf16[2,4,256,256]{3,2,1,0:T(8,128)(2,1)}) %all-gather.4.cloned.1.call-update) | async-done | bytes 1048592 | tf_op jit(solution)/shard_map/all_gather | solution.py:103
  235.1 11.7 %convolution_bitcast_fusion = f32[512,256]{1,0:T(8,128)S(1)} fusion(s32[4,256]{1,0:T(4,128)S(1)} %get-tuple-element.12, s32[512]{0:T(512)S(1)} %copy-done.4, s32[4,256]{1,0:T(4,128)S(1)} %get-tuple-element.13, bf16[2,4,256,256]{3,2,1,0:T(8,128)(2,1)} %all-gather.4.cloned.1.call-done), kind=kOutput, calls=%fused_computation.61 | convolution fusion | flops 282066944 | bytes 1058816 | tf_op jit(solution)/shard_map/gkx,gkl->xl/dot_general | solution.py:109
  246.8 10.8 %convolution_bitcast_fusion.2 = f32[512,256]{1,0:T(8,128)S(1)} fusion(s32[4,256]{1,0:T(4,128)S(1)} %get-tuple-element.12, s32[512]{0:T(512)S(1)} %copy-done.4, s32[4,256]{1,0:T(4,128)S(1)} %get-tuple-element.13, bf16[2,4,256,256]{3,2,1,0:T(8,128)(2,1)S(1)} %copy-done.9), kind=kOutput, calls=%fused_computation.63 | convolution fusion | flops 282066944 | bytes 1058816 | tf_op jit(solution)/shard_map/gkx,gkl->xl/dot_general | solution.py:105
  257.6 11.6 %fusion.40 = bf16[512,256]{1,0:T(8,128)(2,1)} fusion(f32[512,256]{1,0:T(8,128)S(1)} %convolution_bitcast_fusion, s32[4,256]{1,0:T(4,128)S(1)} %get-tuple-element.12, s32[512]{0:T(512)S(1)} %copy-done.4, s32[4,256]{1,0:T(4,128)S(1)} %get-tuple-element.13, bf16[2,4,256,256]{3,2,1,0:T(8,128)(2,1)S(1)} %copy-done.9), kind=kOutput, calls=%fused_computation.68 | convolution fusion | flops 282329088 | bytes 1320960 | tf_op jit(solution)/shard_map/gkx,gkl->xl/dot_general | solution.py:108
  269.2 11.4 %fusion.41 = bf16[512,256]{1,0:T(8,128)(2,1)} fusion(f32[512,256]{1,0:T(8,128)S(1)} %convolution_bitcast_fusion.2, s32[4,256]{1,0:T(4,128)S(1)} %get-tuple-element.12, s32[512]{0:T(512)S(1)} %copy-done.4, s32[4,256]{1,0:T(4,128)S(1)} %get-tuple-element.13, bf16[2,4,256,256]{3,2,1,0:T(8,128)(2,1)S(1)} %copy-done.9), kind=kOutput, calls=%fused_computation.69 | convolution fusion | flops 282329088 | bytes 1320960 | tf_op jit(solution)/shard_map/gkx,gkl->xl/dot_general | solution.py:104
  280.5 18.2 %all-reduce.7.cloned.1.call-done = (bf16[512,256]{1,0:T(8,128)(2,1)}, bf16[512,256]{1,0:T(8,128)(2,1)}) async-done(((bf16[512,256]{1,0:T(8,128)(2,1)}, bf16[512,256]{1,0:T(8,128)(2,1)}), (bf16[512,256]{1,0:T(8,128)(2,1)}, bf16[512,256]{1,0:T(8,128)(2,1)})) %all-reduce.7.cloned.1.call-update) | async-done | bytes 524304 | tf_op jit(solution)/shard_map/psum | solution.py:114
  298.8 11.8 %fusion.44 = f32[512,2048]{1,0:T(8,128)S(1)} fusion(bf16[512,256]{1,0:T(8,128)(2,1)} %get-tuple-element.5, s32[256]{0:T(256)S(1)} %copy-done.6, s32[2048]{0:T(1024)S(1)} %add_select_fusion.9, s32[256]{0:T(256)S(1)} %copy-done.8), kind=kOutput, calls=%fused_computation.77 | convolution fusion | flops 550502400 | bytes 4466688 | tf_op jit(solution)/shard_map/dot_general | solution.py:25
  310.5 12.3 %multiply_convert_fusion = bf16[512,2048]{1,0:T(8,128)(2,1)} fusion(f32[512,2048]{1,0:T(8,128)S(1)} %fusion.44, bf16[512,256]{1,0:T(8,128)(2,1)S(1)} %copy-done.10, f32[2048]{0:T(1024)S(1)} %copy-done.12, s32[256]{0:T(256)S(1)} %copy-done.6, s32[2048]{0:T(1024)S(1)} %add_select_fusion.9, s32[256]{0:T(256)S(1)} %copy-done.8), kind=kOutput, calls=%fused_computation | convolution fusion | flops 553648128 | bytes 6572032 | tf_op jit(solution)/shard_map/dot_general | solution.py:25
  (58 shorter events, 3.7 us)
Async XLA Ops:
  6.5 2.8 copy-start
  6.5 128.0 %all-reduce.5.cloned.1.call-start = ((), (), s32[]{:S(2)}) async-start(), calls=%async_computation.4 | async-start | bytes 2097152
  8.7 13.6 %copy-start.5 = (s32[256]{0:T(256)}, s32[256]{0:T(256)S(1)}, u32[]{:S(2)}) copy-start(s32[256]{0:T(256)S(1)} %get-tuple-element.14) | copy-start | bytes 3076
  8.7 13.6 %copy-start.7 = (s32[256]{0:T(256)}, s32[256]{0:T(256)S(1)}, u32[]{:S(2)}) copy-start(s32[256]{0:T(256)S(1)} %get-tuple-element.15) | copy-start | bytes 3076
  9.4 12.9 %copy-start.11 = (f32[2048]{0:T(1024)S(1)}, f32[2048]{0:T(1024)}, u32[]{:S(2)}) copy-start(f32[2048]{0:T(1024)} %param.8) | copy-start | bytes 24580
  22.3 11.2 %copy-start.13 = (s32[8]{0:T(128)S(1)}, s32[8]{0:T(128)}, u32[]{:S(2)}) copy-start(s32[8]{0:T(128)} %param.10) | copy-start | bytes 100
  33.5 33.1 %copy-start.3 = (s32[512]{0:T(512)}, s32[512]{0:T(512)S(1)}, u32[]{:S(2)}) copy-start(s32[512]{0:T(512)S(1)} %add_select_fusion.16) | copy-start | bytes 6148
  33.7 10.6 %copy-start.15 = (bf16[256,512]{1,0:T(8,128)(2,1)S(1)}, bf16[256,512]{1,0:T(8,128)(2,1)}, u32[]{:S(2)}) copy-start(bf16[256,512]{1,0:T(8,128)(2,1)} %convolution_convert_fusion.3) | copy-start | bytes 786436
  78.6 1.2 copy-start.14
  79.8 93.6 %copy-start.1 = (bf16[256,256]{1,0:T(8,128)(2,1)S(1)}, bf16[256,256]{1,0:T(8,128)(2,1)}, u32[]{:S(2)}) copy-start(bf16[256,256]{1,0:T(8,128)(2,1)} %param.12) | copy-start | bytes 393220
  79.8 91.8 %all-gather.6.cloned.1.call-start = ((), (), s32[]{:S(2)}) async-start(), calls=%async_computation.3 | async-start | bytes 2621440 | tf_op jit(solution)/shard_map/all_gather | solution.py:70
  171.6 8.1 %copy-start.2 = (s32[8,16,16]{2,1,0:T(8,128)S(1)}, s32[8,16,16]{2,1,0:T(8,128)}, u32[]{:S(2)}) copy-start(s32[8,16,16]{2,1,0:T(8,128)} %param.13) | copy-start | bytes 24580
  175.1 15.4 %all-to-all-start = ((bf16[4,2,16384]{2,1,0:T(2,128)(2,1)}), bf16[4,2,16384]{2,1,0:T(2,128)(2,1)S(1)}, u32[]{:S(2)}, u32[]{:S(2)}) async-start(bf16[4,2,16384]{2,1,0:T(2,128)(2,1)} %reshape.297), calls=%async_computation | async-start | bytes 524288 | tf_op jit(solution)/shard_map/all_to_all | solution.py:88
  179.7 55.4 %all-gather.4.cloned.1.call-start = ((), (), s32[]{:S(2)}) async-start(), calls=%async_computation.2 | async-start | bytes 1310720 | tf_op jit(solution)/shard_map/all_gather | solution.py:103
  193.7 41.4 %copy-start.4 = (s32[512]{0:T(512)S(1)}, s32[512]{0:T(512)}, u32[]{:S(2)}) copy-start(s32[512]{0:T(512)} %copy-done.3) | copy-start | bytes 6148
  208.8 89.9 %all-reduce.7.cloned.1.call-start = ((), (), s32[]{:S(2)}) async-start(), calls=%async_computation.5 | async-start | bytes 1048576 | tf_op jit(solution)/shard_map/psum | solution.py:114
  235.1 11.7 %copy-start.9 = (bf16[2,4,256,256]{3,2,1,0:T(8,128)(2,1)S(1)}, bf16[2,4,256,256]{3,2,1,0:T(8,128)(2,1)}, u32[]{:S(2)}) copy-start(bf16[2,4,256,256]{3,2,1,0:T(8,128)(2,1)} %all-gather.4.cloned.1.call-done) | copy-start | bytes 3145732
  269.2 29.6 %copy-start.6 = (s32[256]{0:T(256)S(1)}, s32[256]{0:T(256)}, u32[]{:S(2)}) copy-start(s32[256]{0:T(256)} %copy-done.5) | copy-start | bytes 3076
  269.2 29.6 %copy-start.8 = (s32[256]{0:T(256)S(1)}, s32[256]{0:T(256)}, u32[]{:S(2)}) copy-start(s32[256]{0:T(256)} %copy-done.7) | copy-start | bytes 3076
  298.7 11.8 %copy-start.10 = (bf16[512,256]{1,0:T(8,128)(2,1)S(1)}, bf16[512,256]{1,0:T(8,128)(2,1)}, u32[]{:S(2)}) copy-start(bf16[512,256]{1,0:T(8,128)(2,1)} %get-tuple-element.6) | copy-start | bytes 786436
  298.7 11.8 %copy-start.12 = (f32[2048]{0:T(1024)S(1)}, f32[2048]{0:T(1024)}, u32[]{:S(2)}) copy-start(f32[2048]{0:T(1024)} %param.8) | copy-start | bytes 24580
Sparse Core Ops, SparseCore 0:
  79.9 54.6 all-reduce.4
  137.1 34.4 all-gather.5
  209.0 26.1 all-gather.3
  280.7 18.0 all-reduce.6
